TPU v7x, 256 devices: a whole 4x4x8 slice. The times are simulated.
256 devices in a mesh: section: 16 (over y_hi, x, core), slab: 16 (over z, y_lo).
Axes of the slice: x: 4, y: 4 (y_hi: 2, y_lo: 2; y = y_hi * 2 + y_lo), z: 8, core: 2. Of those that a mesh axis runs over, the one named last changes fastest.
Arguments:
- fwd_states: bfloat16 [16, 128, 32, 512], P('section', None, 'slab'), may hold values from -6 to 6
- back_states: bfloat16 [16, 128, 32, 512], P('section', None, 'slab'), may hold values from -6 to 6
- back_grads: bfloat16 [16, 128, 32, 512], P('section', None, 'slab'), may hold values from -6 to 6
- batch_in: bfloat16 [128, 32, 512], P(None, 'slab'), may hold values from -6 to 6
- head_state: bfloat16 [128, 32, 512], P(None, 'slab'), may hold values from -6 to 6
- head_grad: bfloat16 [128, 32, 512], P(None, 'slab'), may hold values from -6 to 6
- couplings: bfloat16 [16, 4, 27, 64, 64], P('section'), may hold values from -0.15625 to 0.15625
Outputs:
- fwd_out: bfloat16 [16, 128, 32, 512], P('section', None, 'slab')
- back_in: bfloat16 [16, 128, 32, 512], P('section', None, 'slab')
- back_grad: bfloat16 [16, 128, 32, 512], P('section', None, 'slab')
All inputs are finite; a program needn't handle non-finite values.
Results may differ from a plain program's by a relative error of at most 0.006.
Values may be sent and summed in bfloat16 or wider, within the bound.
A program may use at most 128 MiB of HBM per device.

v0:
```python
import functools

import jax
import jax.numpy as jnp
from jax import lax
from jax.experimental import pallas as pl
from jax.experimental.pallas import tpu as pltpu
from jax.sharding import PartitionSpec as P

WID = 32
CELLS = 512
HALF = 64
PAIR = 2 * HALF
PAIRS = 2
MESH = pl.DeviceIdType.MESH
BF16 = jnp.bfloat16
F32 = jnp.float32


def swapped(section, slab):
    return (2 * (section // 2) + slab % 2, 2 * (slab // 2) + section % 2)


def lanes(rows):
    return lax.broadcasted_iota(jnp.int32, (rows, CELLS), 1)


def conv_pair(field, weights):
    col = lanes(1) % WID
    left = pltpu.roll(field, 1, 1) * (col >= 1).astype(BF16)
    right = pltpu.roll(field, CELLS - 1, 1) * (col <= WID - 2).astype(BF16)
    operand = jnp.concatenate([left, field, right], 0)
    sums = jnp.dot(weights, operand, preferred_element_type=F32)
    lane = lanes(PAIR)
    above = jnp.where(lane >= WID, pltpu.roll(sums[:PAIR], WID, 1), 0.0)
    below = jnp.where(lane < CELLS - WID, pltpu.roll(sums[2 * PAIR :], CELLS - WID, 1), 0.0)
    return sums[PAIR : 2 * PAIR] + above + below


def silu_slope(z):
    sig = jax.nn.sigmoid(z)
    return z * sig, sig * (1.0 + z * (1.0 - sig))


def step_kernel(
    n_section, n_slab,
    fwd_ref, state_ref, grad_ref, batch_ref, head_ref, head_grad_ref, kern_ref,
    out_fwd, out_back, out_grad,
    raw, kern, toep, toep_t,
    y1w, y2w, g2w, x1w, x2w, b_x2, b_u, b_w, b_x1, c_x2, c_u, c_w, f_y1, f_y2, d_y1, h2, stage,
    init_send, init_recv, halo_send, halo_recv, out_send, out_recv, kern_sem,
):
    a, b = lax.axis_index("section"), lax.axis_index("slab")
    section, slab = swapped(a, b)
    home_here = a % 2 == b % 2
    has_lo, has_hi = slab > 0, slab < n_slab - 1
    lo_dev, hi_dev = swapped(section, slab - 1), swapped(section, slab + 1)
    up_dev = swapped((a + 1) % n_section, b)
    down_dev = swapped((a + n_section - 1) % n_section, b)

    kern_local = pltpu.make_async_copy(kern_ref, kern, kern_sem.at[0])
    kern_remote = pltpu.make_async_remote_copy(
        kern_ref, kern, kern_sem.at[1], kern_sem.at[2],
        device_id=(a + 1 - 2 * (a % 2), b), device_id_type=MESH,
    )
    pl.when(home_here)(kern_local.start)

    barrier = pltpu.get_barrier_semaphore()

    def greet(device):
        pl.semaphore_signal(barrier, inc=1, device_id=device, device_id_type=MESH)

    greet(((section + n_section - 1) % n_section, slab))
    greet(((section + 1) % n_section, slab))
    pl.when(has_lo)(lambda: greet(lo_dev))
    pl.when(has_hi)(lambda: greet(hi_dev))
    pl.when(jnp.logical_not(home_here))(lambda: greet((section, slab)))
    peers = [has_lo, has_hi, jnp.logical_not(home_here)]
    pl.semaphore_wait(barrier, 2 + sum(peer.astype(jnp.int32) for peer in peers))

    def init_copy(index, source, device):
        half = index % 2
        return pltpu.make_async_remote_copy(
            source.at[pl.ds(half * HALF, HALF)], raw.at[index], init_send.at[index], init_recv.at[index],
            device_id=device, device_id_type=MESH,
        )

    for index, usual, other, device, is_end in (
        (0, state_ref, head_ref, down_dev, a == 0),
        (1, state_ref, head_ref, down_dev, a == 0),
        (3, grad_ref, head_grad_ref, down_dev, a == 0),
        (2, grad_ref, head_grad_ref, down_dev, a == 0),
        (5, fwd_ref, batch_ref, up_dev, a == n_section - 1),
        (4, fwd_ref, batch_ref, up_dev, a == n_section - 1),
    ):
        pl.when(is_end)(init_copy(index, other, device).start)
        pl.when(jnp.logical_not(is_end))(init_copy(index, usual, device).start)

    pl.when(home_here)(kern_remote.start)

    row = lax.broadcasted_iota(jnp.int32, (PAIR, PAIR), 0)
    col = lax.broadcasted_iota(jnp.int32, (PAIR, PAIR), 1)
    split = (col == 2 * (row % HALF) + row // HALF).astype(BF16)
    eye = (row == col).astype(BF16)[:HALF, :HALF]

    for ref, width in ((y1w, 2), (y2w, 1), (g2w, 1), (x2w, 2), (x1w, 1), (b_w, 2), (b_x1, 2), (f_y2, 2), (c_w, 1)):
        rows = width * HALF
        zero = jnp.zeros((rows, CELLS), BF16)

        @pl.when(jnp.logical_not(has_lo))
        def _():
            ref[:rows] = zero

        @pl.when(jnp.logical_not(has_hi))
        def _():
            ref[rows + PAIR :] = zero

    pl.when(home_here)(kern_local.wait)
    pl.when(jnp.logical_not(home_here))(kern_remote.wait_recv)

    def band(step, carry):
        which, b_off = step // 3, step % 3
        blank = jnp.zeros((HALF, HALF), BF16)
        for c_off in range(3):
            taps = [kern[which, 9 * depth + 3 * b_off + c_off] for depth in range(3)]
            line = jnp.concatenate(taps, 1)
            back = [kern[which, 26 - (9 * depth + 3 * b_off + c_off)] for depth in range(3)]
            line_t = lax.dot_general(
                eye, jnp.concatenate(back, 0), (((1,), (1,)), ((), ())), preferred_element_type=F32
            ).astype(BF16)
            for plane in range(2):
                where = (which, pl.ds(pl.multiple_of(b_off * PAIR, PAIR) + plane * HALF, HALF), pl.ds(c_off * 256, 256))
                order = (lambda t: [t, blank]) if plane == 0 else (lambda t: [blank, t])
                toep[where] = jnp.concatenate(order(line), 1)
                toep_t[where] = jnp.concatenate(order(line_t), 1)
        return carry

    lax.fori_loop(0, 6 * PAIRS, band, 0)

    def halo(index, ref, width):
        rows = width * HALF

        def copy(side, source, target, device):
            return pltpu.make_async_remote_copy(
                ref.at[pl.ds(source, rows)], ref.at[pl.ds(target, rows)],
                halo_send.at[index, side], halo_recv.at[index, side],
                device_id=device, device_id_type=MESH,
            )

        low = copy(0, rows, rows + PAIR, lo_dev)
        high = copy(1, PAIR, 0, hi_dev)
        return low, high

    def halo_start(*spec):
        low, high = halo(*spec)
        pl.when(has_lo)(low.start)
        pl.when(has_hi)(high.start)

    def halo_wait(*spec):
        low, high = halo(*spec)
        pl.when(has_lo)(high.wait_recv)
        pl.when(has_hi)(low.wait_recv)

    def halo_done(*spec):
        low, high = halo(*spec)
        pl.when(has_lo)(low.wait_send)
        pl.when(has_hi)(high.wait_send)

    def arrived(index):
        init_copy(index, state_ref, down_dev).wait_recv()
        return jnp.dot(split, raw[index].reshape(PAIR, CELLS), preferred_element_type=F32)

    def out_copy(index, out, half):
        local = pltpu.make_async_copy(stage.at[index], out.at[half], out_send.at[index])
        remote = pltpu.make_async_remote_copy(
            stage.at[index], out.at[half], out_send.at[index], out_recv.at[index],
            device_id=(section, slab), device_id_type=MESH,
        )
        return local, remote

    outs = ((out_fwd, 0), (out_fwd, 1), (out_back, 0), (out_back, 1), (out_grad, 0), (out_grad, 1))

    def out_start(index, value):
        stage[index] = value
        local, remote = out_copy(index, *outs[index])
        pl.when(home_here)(local.start)
        pl.when(jnp.logical_not(home_here))(remote.start)

    edge_row = lax.broadcasted_iota(jnp.int32, (PAIR, CELLS), 0)
    outside = (
        jnp.logical_and(edge_row < HALF, jnp.logical_not(has_lo)),
        jnp.logical_and(edge_row >= HALF, jnp.logical_not(has_hi)),
    )

    def inside(side, value):
        return jnp.where(outside[side], 0.0, value).astype(BF16)

    halos = {
        "y1": (0, y1w, 2), "y2": (1, y2w, 1), "g2": (2, g2w, 1), "x2": (3, x2w, 2), "x1": (4, x1w, 1),
        "w": (5, b_w, 2), "bx1": (6, b_x1, 2), "fy2": (7, f_y2, 2), "cw": (8, c_w, 1),
    }

    y1w[PAIR : 2 * PAIR] = arrived(0).astype(BF16)
    halo_start(*halos["y1"])
    y2w[HALF : HALF + PAIR] = arrived(1).astype(BF16)
    halo_start(*halos["y2"])
    g2w[HALF : HALF + PAIR] = arrived(3).astype(BF16)
    halo_start(*halos["g2"])
    h1 = arrived(2)

    def backward_head(pair, upper, lower, lower_grad, second, inner):
        for side in range(2):
            rows = pl.ds(side * PAIR, PAIR)
            zeta = conv_pair(upper[pl.ds(side * PAIR, 4 * HALF)], toep[2 * pair + 1])
            silu, slope = silu_slope(zeta)
            second[rows] = inside(side, lower[rows].astype(F32) - silu)
            inner[rows] = inside(side, slope * lower_grad(side))

    def backward_tail(pair, upper, second, inner, grad_up):
        silu, slope = silu_slope(conv_pair(second[...], toep[2 * pair]))
        first = (upper[PAIR : 2 * PAIR].astype(F32) - silu).astype(BF16)
        grad_up = grad_up + conv_pair(inner[...], toep_t[2 * pair + 1])
        return first, grad_up, (slope * grad_up).astype(BF16)

    def forward(pair, upper, lower, mixed):
        for side in range(2):
            rows = pl.ds(side * PAIR, PAIR)
            zeta = conv_pair(lower[pl.ds(side * PAIR, 4 * HALF)], toep[2 * pair])
            mixed[rows] = inside(side, upper[rows].astype(F32) + silu_slope(zeta)[0])
        zeta = conv_pair(mixed[...], toep[2 * pair + 1])
        return (lower[PAIR : 2 * PAIR].astype(F32) + silu_slope(zeta)[0]).astype(BF16)

    for name in ("y1", "y2", "g2"):
        halo_wait(*halos[name])
    backward_head(1, y1w, y2w, lambda side: g2w[pl.ds(side * PAIR, PAIR)].astype(F32), b_x2, b_u)
    first, h1, inner_w = backward_tail(1, y1w, b_x2, b_u, h1)
    b_w[PAIR : 2 * PAIR] = inner_w
    halo_start(*halos["w"])
    b_x1[PAIR : 2 * PAIR] = first
    halo_start(*halos["bx1"])

    x2w[PAIR : 2 * PAIR] = arrived(5).astype(BF16)
    halo_start(*halos["x2"])
    x1w[HALF : HALF + PAIR] = arrived(4).astype(BF16)
    halo_start(*halos["x1"])
    halo_wait(*halos["x2"])
    halo_wait(*halos["x1"])
    f_y2[PAIR : 2 * PAIR] = forward(0, x1w, x2w, f_y1)
    halo_start(*halos["fy2"])

    halo_wait(*halos["w"])
    for side in range(2):
        rows = pl.ds(side * PAIR, PAIR)
        h2[rows] = g2w[rows].astype(F32) + conv_pair(b_w[pl.ds(side * PAIR, 4 * HALF)], toep_t[2])
    halo_wait(*halos["bx1"])
    backward_head(0, b_x1, b_x2, lambda side: h2[pl.ds(side * PAIR, PAIR)], c_x2, c_u)
    first, h1, inner_w = backward_tail(0, b_x1, c_x2, c_u, h1)
    c_w[HALF : HALF + PAIR] = inner_w
    halo_start(*halos["cw"])
    out_start(2, first)
    out_start(3, c_x2[HALF : HALF + PAIR])
    out_start(4, h1.astype(BF16))

    halo_wait(*halos["fy2"])
    lower = forward(1, f_y1, f_y2, d_y1)
    out_start(0, d_y1[HALF : HALF + PAIR])
    out_start(1, lower)

    halo_wait(*halos["cw"])
    out_start(5, (h2[HALF : HALF + PAIR] + conv_pair(c_w[...], toep_t[0])).astype(BF16))

    for index in range(6):
        init_copy(index, state_ref, down_dev).wait_send()
        local, remote = out_copy(index, *outs[index])
        pl.when(home_here)(local.wait)
        pl.when(jnp.logical_not(home_here))(remote.wait)
    pl.when(home_here)(kern_remote.wait_send)
    for spec in halos.values():
        halo_done(*spec)


def shards(fwd_states, back_states, back_grads, batch_in, head_state, head_grad, couplings):
    n_section, n_slab = lax.axis_size("section"), lax.axis_size("slab")
    anywhere = pl.BlockSpec(memory_space=pl.ANY)
    field = lambda planes: pltpu.VMEM((planes * HALF, CELLS), BF16)
    dma = pltpu.SemaphoreType.DMA
    out = jax.ShapeDtypeStruct((2, PAIR, CELLS), BF16)
    results = pl.pallas_call(
        functools.partial(step_kernel, n_section, n_slab),
        out_shape=(out, out, out),
        in_specs=[anywhere] * 7,
        out_specs=(anywhere,) * 3,
        scratch_shapes=[
            pltpu.VMEM((6, HALF, 2, CELLS), BF16),
            pltpu.VMEM(couplings.shape[1:], BF16),
            pltpu.VMEM((2 * PAIRS, 3 * PAIR, 12 * HALF), BF16),
            pltpu.VMEM((2 * PAIRS, 3 * PAIR, 12 * HALF), BF16),
            field(6), field(4), field(4), field(4), field(6),
            field(4), field(4), field(6), field(6),
            field(4), field(4), field(4),
            field(4), field(6), field(4),
            pltpu.VMEM((2 * PAIR, CELLS), F32),
            pltpu.VMEM((6, PAIR, CELLS), BF16),
            dma((6,)), dma((6,)), dma((9, 2)), dma((9, 2)), dma((6,)), dma((6,)), dma((3,)),
        ],
        compiler_params=pltpu.CompilerParams(collective_id=0, has_side_effects=True),
    )(fwd_states[0], back_states[0], back_grads[0], batch_in, head_state, head_grad, couplings[0])

    def placed(value):
        planes = value.reshape(2, 2, HALF, CELLS)
        return jnp.transpose(planes, (0, 2, 1, 3)).reshape(1, 2 * HALF, 2, CELLS)

    return tuple(placed(value) for value in results)


def solution(mesh):
    return jax.shard_map(
        shards,
        mesh=mesh,
        in_specs=(
            P("section", None, "slab", None),
            P("section", None, "slab", None),
            P("section", None, "slab", None),
            P(None, "slab", None),
            P(None, "slab", None),
            P(None, "slab", None),
            P("section", None, None, None, None),
        ),
        out_specs=(
            P("section", None, "slab", None),
            P("section", None, "slab", None),
            P("section", None, "slab", None),
        ),
        check_vma=False,
    )
```

profile of v0, /device:TPU:126, one launch (start us, length us, event | category | flops | bytes accessed | tf_op | source)
XLA Modules:
  0.0 53.7 jit_solution(15095881021433957480)
XLA Ops:
  0.6 47.3 %shard_map.94 = (bf16[2,128,512]{2,1,0:T(8,128)(2,1)}, bf16[2,128,512]{2,1,0:T(8,128)(2,1)}, bf16[2,128,512]{2,1,0:T(8,128)(2,1)}) custom-call(bf16[128,2,512]{2,1,0:T(2,128)(2,1)} %bitcast.17, bf16[128,2,512]{2,1,0:T(2,128)(2,1)} %bitcast.18, bf16[128,2,512]{2,1,0:T(2,128)(2,1)} %bitcast.19, bf16[128,2,512]{2,1,0:T(2,128)(2,1)} %batch_ref.1, ...), custom_call_target="tpu_custom_call" | custom-call | tf_op jit(solution)/shard_map/pallas_call | solution.py:288
  47.9 1.9 %copy.10 = bf16[2,64,2,512]{3,2,1,0:T(2,128)(2,1)} copy(bf16[2,64,2,512]{3,1,2,0:T(8,128)(2,1)} %bitcast.25) | data formatting | bytes 524288 | tf_op jit(solution)/shard_map/transpose | solution.py:311
  49.8 1.9 %copy.11 = bf16[2,64,2,512]{3,2,1,0:T(2,128)(2,1)} copy(bf16[2,64,2,512]{3,1,2,0:T(8,128)(2,1)} %bitcast.24) | data formatting | bytes 524288 | tf_op jit(solution)/shard_map/transpose | solution.py:311
  51.8 1.9 %copy.12 = bf16[2,64,2,512]{3,2,1,0:T(2,128)(2,1)} copy(bf16[2,64,2,512]{3,1,2,0:T(8,128)(2,1)} %bitcast.23) | data formatting | bytes 524288 | tf_op jit(solution)/shard_map/transpose | solution.py:311
where the time goes:
time: 53.9 us; the launch traced here: 53.7 us
  Pallas kernels  47.3 us (88%)
  local copies, waits for them, and re-layouts  5.77 us (11%)
  between operations  0.64 us (1%)
    pallas_call x1, Pallas kernels, shards(): pl.pallas_call(functools.partial(step_kernel, n_section, n_slab), out_sha...  47.3 us
    transpose x3, local copies, waits for them, and re-layouts, placed(): return jnp.transpose(planes, (0, 2, 1, 3)).reshape(1, 2 * HALF, 2, CELLS)  5.77 us

commit v1 on v0

--- a/solution.py
+++ b/solution.py
@@ -47,7 +47,7 @@
     fwd_ref, state_ref, grad_ref, batch_ref, head_ref, head_grad_ref, kern_ref,
     out_fwd, out_back, out_grad,
     raw, kern, toep, toep_t,
-    y1w, y2w, g2w, x1w, x2w, b_x2, b_u, b_w, b_x1, c_x2, c_u, c_w, f_y1, f_y2, d_y1, h2, stage,
+    y1w, y2w, g2w, x1w, x2w, b_x2, b_u, b_w, b_x1, c_x2, c_u, c_w, f_y1, f_y2, d_y1, h2, zeta, stage,
     init_send, init_recv, halo_send, halo_recv, out_send, out_recv, kern_sem,
 ):
     a, b = lax.axis_index("section"), lax.axis_index("slab")
@@ -55,8 +55,7 @@
     home_here = a % 2 == b % 2
     has_lo, has_hi = slab > 0, slab < n_slab - 1
     lo_dev, hi_dev = swapped(section, slab - 1), swapped(section, slab + 1)
-    up_dev = swapped((a + 1) % n_section, b)
-    down_dev = swapped((a + n_section - 1) % n_section, b)
+    up_dev, down_dev = swapped(a + 1, b), swapped(a - 1, b)
 
     kern_local = pltpu.make_async_copy(kern_ref, kern, kern_sem.at[0])
     kern_remote = pltpu.make_async_remote_copy(
@@ -70,13 +69,13 @@
     def greet(device):
         pl.semaphore_signal(barrier, inc=1, device_id=device, device_id_type=MESH)
 
-    greet(((section + n_section - 1) % n_section, slab))
-    greet(((section + 1) % n_section, slab))
+    greet((jnp.where(section == 0, 1, section - 1), slab))
+    greet((jnp.where(section == n_section - 1, n_section - 2, section + 1), slab))
     pl.when(has_lo)(lambda: greet(lo_dev))
     pl.when(has_hi)(lambda: greet(hi_dev))
     pl.when(jnp.logical_not(home_here))(lambda: greet((section, slab)))
-    peers = [has_lo, has_hi, jnp.logical_not(home_here)]
-    pl.semaphore_wait(barrier, 2 + sum(peer.astype(jnp.int32) for peer in peers))
+    peers = [has_lo, has_hi, jnp.logical_not(home_here), a > 0, a < n_section - 1, a == 1, a == n_section - 2]
+    pl.semaphore_wait(barrier, sum(peer.astype(jnp.int32) for peer in peers))
 
     def init_copy(index, source, device):
         half = index % 2
@@ -85,22 +84,28 @@
             device_id=device, device_id_type=MESH,
         )
 
-    for index, usual, other, device, is_end in (
-        (0, state_ref, head_ref, down_dev, a == 0),
-        (1, state_ref, head_ref, down_dev, a == 0),
-        (3, grad_ref, head_grad_ref, down_dev, a == 0),
-        (2, grad_ref, head_grad_ref, down_dev, a == 0),
-        (5, fwd_ref, batch_ref, up_dev, a == n_section - 1),
-        (4, fwd_ref, batch_ref, up_dev, a == n_section - 1),
-    ):
-        pl.when(is_end)(init_copy(index, other, device).start)
-        pl.when(jnp.logical_not(is_end))(init_copy(index, usual, device).start)
-
+    def init_start(index, source, edge_source, device, edge_device, last, edge):
+        pl.when(jnp.logical_not(last))(init_copy(index, source, device).start)
+        pl.when(edge)(init_copy(index, edge_source, edge_device).start)
+
+    def init_done(index, device, edge_device, last, edge):
+        pl.when(jnp.logical_not(last))(init_copy(index, state_ref, device).wait_send)
+        pl.when(edge)(init_copy(index, state_ref, edge_device).wait_send)
+
+    down = (down_dev, swapped(n_section - 1, b), a == 0, a == n_section - 2)
+    up = (up_dev, swapped(0, b), a == n_section - 1, a == 1)
+    for index, source, edge_source in ((0, state_ref, head_ref), (1, state_ref, head_ref), (3, grad_ref, head_grad_ref)):
+        init_start(index, source, edge_source, *down)
+
+    def forward_start():
+        for index in (5, 4):
+            init_start(index, fwd_ref, batch_ref, *up)
     pl.when(home_here)(kern_remote.start)
 
     row = lax.broadcasted_iota(jnp.int32, (PAIR, PAIR), 0)
     col = lax.broadcasted_iota(jnp.int32, (PAIR, PAIR), 1)
     split = (col == 2 * (row % HALF) + row // HALF).astype(BF16)
+    merge = (col == HALF * (row % 2) + row // 2).astype(BF16)
     eye = (row == col).astype(BF16)[:HALF, :HALF]
 
     for ref, width in ((y1w, 2), (y2w, 1), (g2w, 1), (x2w, 2), (x1w, 1), (b_w, 2), (b_x1, 2), (f_y2, 2), (c_w, 1)):
@@ -117,6 +122,7 @@
 
     pl.when(home_here)(kern_local.wait)
     pl.when(jnp.logical_not(home_here))(kern_remote.wait_recv)
+    pl.when(jnp.logical_not(home_here))(forward_start)
 
     def band(step, carry):
         which, b_off = step // 3, step % 3
@@ -136,6 +142,7 @@
         return carry
 
     lax.fori_loop(0, 6 * PAIRS, band, 0)
+    pl.when(home_here)(forward_start)
 
     def halo(index, ref, width):
         rows = width * HALF
@@ -171,9 +178,9 @@
         return jnp.dot(split, raw[index].reshape(PAIR, CELLS), preferred_element_type=F32)
 
     def out_copy(index, out, half):
-        local = pltpu.make_async_copy(stage.at[index], out.at[half], out_send.at[index])
+        local = pltpu.make_async_copy(stage.at[index], out.at[pl.ds(half * HALF, HALF)], out_send.at[index])
         remote = pltpu.make_async_remote_copy(
-            stage.at[index], out.at[half], out_send.at[index], out_recv.at[index],
+            stage.at[index], out.at[pl.ds(half * HALF, HALF)], out_send.at[index], out_recv.at[index],
             device_id=(section, slab), device_id_type=MESH,
         )
         return local, remote
@@ -181,7 +188,8 @@
     outs = ((out_fwd, 0), (out_fwd, 1), (out_back, 0), (out_back, 1), (out_grad, 0), (out_grad, 1))
 
     def out_start(index, value):
-        stage[index] = value
+        rows = jnp.dot(merge, value, preferred_element_type=F32).astype(BF16)
+        stage[index] = rows.reshape(HALF, 2, CELLS)
         local, remote = out_copy(index, *outs[index])
         pl.when(home_here)(local.start)
         pl.when(jnp.logical_not(home_here))(remote.start)
@@ -204,61 +212,70 @@
     halo_start(*halos["y1"])
     y2w[HALF : HALF + PAIR] = arrived(1).astype(BF16)
     halo_start(*halos["y2"])
+    init_start(2, grad_ref, head_grad_ref, *down)
     g2w[HALF : HALF + PAIR] = arrived(3).astype(BF16)
     halo_start(*halos["g2"])
-    h1 = arrived(2)
-
-    def backward_head(pair, upper, lower, lower_grad, second, inner):
-        for side in range(2):
-            rows = pl.ds(side * PAIR, PAIR)
-            zeta = conv_pair(upper[pl.ds(side * PAIR, 4 * HALF)], toep[2 * pair + 1])
-            silu, slope = silu_slope(zeta)
-            second[rows] = inside(side, lower[rows].astype(F32) - silu)
-            inner[rows] = inside(side, slope * lower_grad(side))
-
-    def backward_tail(pair, upper, second, inner, grad_up):
+    x2w[PAIR : 2 * PAIR] = arrived(5).astype(BF16)
+    halo_start(*halos["x2"])
+
+    sides = [(side, pl.ds(side * PAIR, PAIR), pl.ds(side * PAIR, 4 * HALF)) for side in range(2)]
+
+    def zeta_upper(pair, upper):
+        for side, rows, wide in sides:
+            zeta[rows] = conv_pair(upper[wide], toep[2 * pair + 1])
+
+    def undo_second(lower, second):
+        for side, rows, wide in sides:
+            second[rows] = inside(side, lower[rows].astype(F32) - silu_slope(zeta[rows])[0])
+
+    def undo_first(pair, upper, second):
         silu, slope = silu_slope(conv_pair(second[...], toep[2 * pair]))
-        first = (upper[PAIR : 2 * PAIR].astype(F32) - silu).astype(BF16)
-        grad_up = grad_up + conv_pair(inner[...], toep_t[2 * pair + 1])
-        return first, grad_up, (slope * grad_up).astype(BF16)
+        return (upper[PAIR : 2 * PAIR].astype(F32) - silu).astype(BF16), slope
+
+    def grad_inner(lower_grad, inner):
+        for side, rows, wide in sides:
+            inner[rows] = inside(side, silu_slope(zeta[rows])[1] * lower_grad[rows].astype(F32))
 
     def forward(pair, upper, lower, mixed):
-        for side in range(2):
-            rows = pl.ds(side * PAIR, PAIR)
-            zeta = conv_pair(lower[pl.ds(side * PAIR, 4 * HALF)], toep[2 * pair])
-            mixed[rows] = inside(side, upper[rows].astype(F32) + silu_slope(zeta)[0])
-        zeta = conv_pair(mixed[...], toep[2 * pair + 1])
-        return (lower[PAIR : 2 * PAIR].astype(F32) + silu_slope(zeta)[0]).astype(BF16)
-
-    for name in ("y1", "y2", "g2"):
-        halo_wait(*halos[name])
-    backward_head(1, y1w, y2w, lambda side: g2w[pl.ds(side * PAIR, PAIR)].astype(F32), b_x2, b_u)
-    first, h1, inner_w = backward_tail(1, y1w, b_x2, b_u, h1)
-    b_w[PAIR : 2 * PAIR] = inner_w
-    halo_start(*halos["w"])
+        for side, rows, wide in sides:
+            z = conv_pair(lower[wide], toep[2 * pair])
+            mixed[rows] = inside(side, upper[rows].astype(F32) + silu_slope(z)[0])
+        z = conv_pair(mixed[...], toep[2 * pair + 1])
+        return (lower[PAIR : 2 * PAIR].astype(F32) + silu_slope(z)[0]).astype(BF16)
+
+    halo_wait(*halos["y1"])
+    zeta_upper(1, y1w)
+    x1w[HALF : HALF + PAIR] = arrived(4).astype(BF16)
+    halo_start(*halos["x1"])
+    halo_wait(*halos["y2"])
+    undo_second(y2w, b_x2)
+    first, slope = undo_first(1, y1w, b_x2)
     b_x1[PAIR : 2 * PAIR] = first
     halo_start(*halos["bx1"])
-
-    x2w[PAIR : 2 * PAIR] = arrived(5).astype(BF16)
-    halo_start(*halos["x2"])
-    x1w[HALF : HALF + PAIR] = arrived(4).astype(BF16)
-    halo_start(*halos["x1"])
+    halo_wait(*halos["g2"])
+    grad_inner(g2w, b_u)
+    h1 = conv_pair(b_u[...], toep_t[3]) + arrived(2)
+    b_w[PAIR : 2 * PAIR] = (slope * h1).astype(BF16)
+    halo_start(*halos["w"])
+
     halo_wait(*halos["x2"])
     halo_wait(*halos["x1"])
     f_y2[PAIR : 2 * PAIR] = forward(0, x1w, x2w, f_y1)
     halo_start(*halos["fy2"])
 
+    halo_wait(*halos["bx1"])
+    zeta_upper(0, b_x1)
+    undo_second(b_x2, c_x2)
+    out_start(3, c_x2[HALF : HALF + PAIR])
+    first, slope = undo_first(0, b_x1, c_x2)
+    out_start(2, first)
     halo_wait(*halos["w"])
-    for side in range(2):
-        rows = pl.ds(side * PAIR, PAIR)
-        h2[rows] = g2w[rows].astype(F32) + conv_pair(b_w[pl.ds(side * PAIR, 4 * HALF)], toep_t[2])
-    halo_wait(*halos["bx1"])
-    backward_head(0, b_x1, b_x2, lambda side: h2[pl.ds(side * PAIR, PAIR)], c_x2, c_u)
-    first, h1, inner_w = backward_tail(0, b_x1, c_x2, c_u, h1)
-    c_w[HALF : HALF + PAIR] = inner_w
+    for side, rows, wide in sides:
+        h2[rows] = g2w[rows].astype(F32) + conv_pair(b_w[wide], toep_t[2])
+    grad_inner(h2, c_u)
+    h1 = h1 + conv_pair(c_u[...], toep_t[1])
+    c_w[HALF : HALF + PAIR] = (slope * h1).astype(BF16)
     halo_start(*halos["cw"])
-    out_start(2, first)
-    out_start(3, c_x2[HALF : HALF + PAIR])
     out_start(4, h1.astype(BF16))
 
     halo_wait(*halos["fy2"])
@@ -270,7 +287,7 @@
     out_start(5, (h2[HALF : HALF + PAIR] + conv_pair(c_w[...], toep_t[0])).astype(BF16))
 
     for index in range(6):
-        init_copy(index, state_ref, down_dev).wait_send()
+        init_done(index, *(down if index < 4 else up))
         local, remote = out_copy(index, *outs[index])
         pl.when(home_here)(local.wait)
         pl.when(jnp.logical_not(home_here))(remote.wait)
@@ -279,12 +296,24 @@
         halo_done(*spec)
 
 
+def settle_kernel(in_0, in_1, in_2, out_0, out_1, out_2, buffer, sems):
+    reads = [pltpu.make_async_copy(ref, buffer.at[i], sems.at[0, i]) for i, ref in enumerate((in_0, in_1, in_2))]
+    writes = [pltpu.make_async_copy(buffer.at[i], ref, sems.at[1, i]) for i, ref in enumerate((out_0, out_1, out_2))]
+    for copy in reads:
+        copy.start()
+    for read, write in zip(reads, writes):
+        read.wait()
+        write.start()
+    for copy in writes:
+        copy.wait()
+
+
 def shards(fwd_states, back_states, back_grads, batch_in, head_state, head_grad, couplings):
     n_section, n_slab = lax.axis_size("section"), lax.axis_size("slab")
     anywhere = pl.BlockSpec(memory_space=pl.ANY)
     field = lambda planes: pltpu.VMEM((planes * HALF, CELLS), BF16)
     dma = pltpu.SemaphoreType.DMA
-    out = jax.ShapeDtypeStruct((2, PAIR, CELLS), BF16)
+    out = jax.ShapeDtypeStruct((PAIR, 2, CELLS), BF16)
     results = pl.pallas_call(
         functools.partial(step_kernel, n_section, n_slab),
         out_shape=(out, out, out),
@@ -300,17 +329,21 @@
             field(4), field(4), field(4),
             field(4), field(6), field(4),
             pltpu.VMEM((2 * PAIR, CELLS), F32),
-            pltpu.VMEM((6, PAIR, CELLS), BF16),
+            pltpu.VMEM((2 * PAIR, CELLS), F32),
+            pltpu.VMEM((6, HALF, 2, CELLS), BF16),
             dma((6,)), dma((6,)), dma((9, 2)), dma((9, 2)), dma((6,)), dma((6,)), dma((3,)),
         ],
         compiler_params=pltpu.CompilerParams(collective_id=0, has_side_effects=True),
     )(fwd_states[0], back_states[0], back_grads[0], batch_in, head_state, head_grad, couplings[0])
 
-    def placed(value):
-        planes = value.reshape(2, 2, HALF, CELLS)
-        return jnp.transpose(planes, (0, 2, 1, 3)).reshape(1, 2 * HALF, 2, CELLS)
-
-    return tuple(placed(value) for value in results)
+    settled = pl.pallas_call(
+        settle_kernel,
+        out_shape=(out, out, out),
+        in_specs=[anywhere] * 3,
+        out_specs=(anywhere,) * 3,
+        scratch_shapes=[pltpu.VMEM((3, PAIR, 2, CELLS), BF16), dma((2, 3))],
+    )(*results)
+    return tuple(value[None] for value in settled)
 
 
 def solution(mesh):

time: 53.9 us -> 40.9 us (0.76)
  Pallas kernels: 47.3 us -> 40.1 us
  local copies, waits for them, and re-layouts: 5.77 us -> 0 us
    pallas_call x1, Pallas kernels: 47.3 us -> 38.2 us  [shards(): pl.pallas_call(functools.partial(step_kernel, n_section, n_slab), out_sha...]
    transpose x3 -> x0, local copies, waits for them, and re-layouts: 5.77 us -> none  [placed(): return jnp.transpose(planes, (0, 2, 1, 3)).reshape(1, 2 * HALF, 2, CELLS)]
    pallas_call x0 -> x1, Pallas kernels: none -> 1.88 us  [shards(): pl.pallas_call(settle_kernel, out_shape=(out, out, out), in_specs=[anywhe...]
where the time goes in v1:
time: 40.9 us; the launch traced here: 40.8 us
  Pallas kernels  40.1 us (98%)
  between operations  0.64 us (2%)
    pallas_call x1, Pallas kernels, shards(): pl.pallas_call(functools.partial(step_kernel, n_section, n_slab), out_sha...  38.2 us
    pallas_call x1, Pallas kernels, shards(): pl.pallas_call(settle_kernel, out_shape=(out, out, out), in_specs=[anywhe...  1.88 us

profile of v1, /device:TPU:126, one launch (start us, length us, event | category | flops | bytes accessed | tf_op | source)
XLA Modules:
  0.0 40.8 jit_solution(11482597687323097635)
XLA Ops:
  0.6 38.2 %shard_map.94 = (bf16[128,2,512]{2,1,0:T(2,128)(2,1)}, bf16[128,2,512]{2,1,0:T(2,128)(2,1)}, bf16[128,2,512]{2,1,0:T(2,128)(2,1)}) custom-call(bf16[128,2,512]{2,1,0:T(2,128)(2,1)} %bitcast.8, bf16[128,2,512]{2,1,0:T(2,128)(2,1)} %bitcast.9, bf16[128,2,512]{2,1,0:T(2,128)(2,1)} %bitcast.10, bf16[128,2,512]{2,1,0:T(2,128)(2,1)} %batch_ref.1, ...), custom_call_target="tpu_custom_call" | custom-call | tf_op jit(solution)/shard_map/pallas_call | solution.py:317
  38.9 1.9 %shard_map.95 = (bf16[128,2,512]{2,1,0:T(2,128)(2,1)}, bf16[128,2,512]{2,1,0:T(2,128)(2,1)}, bf16[128,2,512]{2,1,0:T(2,128)(2,1)}) custom-call(bf16[128,2,512]{2,1,0:T(2,128)(2,1)} %get-tuple-element.9.in_0, bf16[128,2,512]{2,1,0:T(2,128)(2,1)} %get-tuple-element.10.in_1, bf16[128,2,512]{2,1,0:T(2,128)(2,1)} %get-tuple-element.11.in_2), custom_call_target="tpu_custom_call" | custom-call | tf_op jit(solution)/shard_map/pallas_call | solution.py:339

commit v2 on v1

--- a/solution.py
+++ b/solution.py
@@ -12,6 +12,7 @@
 HALF = 64
 PAIR = 2 * HALF
 PAIRS = 2
+RELAYED = (1, 2, 3)
 MESH = pl.DeviceIdType.MESH
 BF16 = jnp.bfloat16
 F32 = jnp.float32
@@ -46,9 +47,9 @@
     n_section, n_slab,
     fwd_ref, state_ref, grad_ref, batch_ref, head_ref, head_grad_ref, kern_ref,
     out_fwd, out_back, out_grad,
-    raw, kern, toep, toep_t,
+    raw, relay, kern, toep, toep_t,
     y1w, y2w, g2w, x1w, x2w, b_x2, b_u, b_w, b_x1, c_x2, c_u, c_w, f_y1, f_y2, d_y1, h2, zeta, stage,
-    init_send, init_recv, halo_send, halo_recv, out_send, out_recv, kern_sem,
+    init_send, init_recv, relay_send, relay_recv, halo_send, halo_recv, out_send, out_recv, kern_sem,
 ):
     a, b = lax.axis_index("section"), lax.axis_index("slab")
     section, slab = swapped(a, b)
@@ -64,6 +65,12 @@
     )
     pl.when(home_here)(kern_local.start)
 
+    mid = n_section // 2
+    odd_slab = b % 2 == 1
+    sends_relayed = jnp.logical_and(a == mid, odd_slab)
+    relays = jnp.logical_and(a == mid - 1, jnp.logical_not(odd_slab))
+    gets_relayed = jnp.logical_and(a == mid - 1, odd_slab)
+
     barrier = pltpu.get_barrier_semaphore()
 
     def greet(device):
@@ -71,10 +78,13 @@
 
     greet((jnp.where(section == 0, 1, section - 1), slab))
     greet((jnp.where(section == n_section - 1, n_section - 2, section + 1), slab))
+    pl.when(relays)(lambda: greet((a + 1, b + 1)))
+    pl.when(gets_relayed)(lambda: greet((a, b - 1)))
     pl.when(has_lo)(lambda: greet(lo_dev))
     pl.when(has_hi)(lambda: greet(hi_dev))
     pl.when(jnp.logical_not(home_here))(lambda: greet((section, slab)))
     peers = [has_lo, has_hi, jnp.logical_not(home_here), a > 0, a < n_section - 1, a == 1, a == n_section - 2]
+    peers += [sends_relayed, relays]
     pl.semaphore_wait(barrier, sum(peer.astype(jnp.int32) for peer in peers))
 
     def init_copy(index, source, device):
@@ -84,7 +94,29 @@
             device_id=device, device_id_type=MESH,
         )
 
+    def relay_in(index, source):
+        half = index % 2
+        return pltpu.make_async_remote_copy(
+            source.at[pl.ds(half * HALF, HALF)], relay.at[index], init_send.at[index], relay_recv.at[index],
+            device_id=(a - 1, b - 1), device_id_type=MESH,
+        )
+
+    def relay_out(index):
+        return pltpu.make_async_remote_copy(
+            relay.at[index], raw.at[index], relay_send.at[index], init_recv.at[index],
+            device_id=(a, b + 1), device_id_type=MESH,
+        )
+
+    def relay_on(index):
+        @pl.when(relays)
+        def _():
+            relay_in(index, state_ref).wait_recv()
+            relay_out(index).start()
+
     def init_start(index, source, edge_source, device, edge_device, last, edge):
+        if index in RELAYED:
+            last = jnp.logical_or(last, sends_relayed)
+            pl.when(sends_relayed)(relay_in(index, source).start)
         pl.when(jnp.logical_not(last))(init_copy(index, source, device).start)
         pl.when(edge)(init_copy(index, edge_source, edge_device).start)
 
@@ -212,9 +244,11 @@
     halo_start(*halos["y1"])
     y2w[HALF : HALF + PAIR] = arrived(1).astype(BF16)
     halo_start(*halos["y2"])
+    relay_on(1)
     init_start(2, grad_ref, head_grad_ref, *down)
     g2w[HALF : HALF + PAIR] = arrived(3).astype(BF16)
     halo_start(*halos["g2"])
+    relay_on(3)
     x2w[PAIR : 2 * PAIR] = arrived(5).astype(BF16)
     halo_start(*halos["x2"])
 
@@ -236,10 +270,11 @@
         for side, rows, wide in sides:
             inner[rows] = inside(side, silu_slope(zeta[rows])[1] * lower_grad[rows].astype(F32))
 
-    def forward(pair, upper, lower, mixed):
+    def forward(pair, upper, lower, mixed, ready=lambda: None):
         for side, rows, wide in sides:
             z = conv_pair(lower[wide], toep[2 * pair])
             mixed[rows] = inside(side, upper[rows].astype(F32) + silu_slope(z)[0])
+        ready()
         z = conv_pair(mixed[...], toep[2 * pair + 1])
         return (lower[PAIR : 2 * PAIR].astype(F32) + silu_slope(z)[0]).astype(BF16)
 
@@ -252,6 +287,7 @@
     first, slope = undo_first(1, y1w, b_x2)
     b_x1[PAIR : 2 * PAIR] = first
     halo_start(*halos["bx1"])
+    relay_on(2)
     halo_wait(*halos["g2"])
     grad_inner(g2w, b_u)
     h1 = conv_pair(b_u[...], toep_t[3]) + arrived(2)
@@ -279,15 +315,15 @@
     out_start(4, h1.astype(BF16))
 
     halo_wait(*halos["fy2"])
-    lower = forward(1, f_y1, f_y2, d_y1)
-    out_start(0, d_y1[HALF : HALF + PAIR])
-    out_start(1, lower)
+    out_start(1, forward(1, f_y1, f_y2, d_y1, lambda: out_start(0, d_y1[HALF : HALF + PAIR])))
 
     halo_wait(*halos["cw"])
     out_start(5, (h2[HALF : HALF + PAIR] + conv_pair(c_w[...], toep_t[0])).astype(BF16))
 
     for index in range(6):
         init_done(index, *(down if index < 4 else up))
+        if index in RELAYED:
+            pl.when(relays)(relay_out(index).wait_send)
         local, remote = out_copy(index, *outs[index])
         pl.when(home_here)(local.wait)
         pl.when(jnp.logical_not(home_here))(remote.wait)
@@ -321,6 +357,7 @@
         out_specs=(anywhere,) * 3,
         scratch_shapes=[
             pltpu.VMEM((6, HALF, 2, CELLS), BF16),
+            pltpu.VMEM((4, HALF, 2, CELLS), BF16),
             pltpu.VMEM(couplings.shape[1:], BF16),
             pltpu.VMEM((2 * PAIRS, 3 * PAIR, 12 * HALF), BF16),
             pltpu.VMEM((2 * PAIRS, 3 * PAIR, 12 * HALF), BF16),
@@ -331,7 +368,7 @@
             pltpu.VMEM((2 * PAIR, CELLS), F32),
             pltpu.VMEM((2 * PAIR, CELLS), F32),
             pltpu.VMEM((6, HALF, 2, CELLS), BF16),
-            dma((6,)), dma((6,)), dma((9, 2)), dma((9, 2)), dma((6,)), dma((6,)), dma((3,)),
+            dma((6,)), dma((6,)), dma((4,)), dma((4,)), dma((9, 2)), dma((9, 2)), dma((6,)), dma((6,)), dma((3,)),
         ],
         compiler_params=pltpu.CompilerParams(collective_id=0, has_side_effects=True),
     )(fwd_states[0], back_states[0], back_grads[0], batch_in, head_state, head_grad, couplings[0])

time: 40.9 us -> 37.4 us (0.914)
  the two profiles are of different devices: /device:TPU:126 before, /device:TPU:129 now
where the time goes in v2:
time: 37.4 us; the launch traced here: 37.3 us
  Pallas kernels  36.7 us (98%)
  between operations  0.64 us (2%)
    pallas_call x1, Pallas kernels, shards(): pl.pallas_call(functools.partial(step_kernel, n_section, n_slab), out_sha...  34.8 us
    pallas_call x1, Pallas kernels, shards(): pl.pallas_call(settle_kernel, out_shape=(out, out, out), in_specs=[anywhe...  1.88 us

profile of v2, /device:TPU:129, one launch (start us, length us, event | category | flops | bytes accessed | tf_op | source)
XLA Modules:
  0.0 37.3 jit_solution(1464938141322363269)
XLA Ops:
  0.6 34.8 %shard_map.94 = (bf16[128,2,512]{2,1,0:T(2,128)(2,1)}, bf16[128,2,512]{2,1,0:T(2,128)(2,1)}, bf16[128,2,512]{2,1,0:T(2,128)(2,1)}) custom-call(bf16[128,2,512]{2,1,0:T(2,128)(2,1)} %bitcast.8, bf16[128,2,512]{2,1,0:T(2,128)(2,1)} %bitcast.9, bf16[128,2,512]{2,1,0:T(2,128)(2,1)} %bitcast.10, bf16[128,2,512]{2,1,0:T(2,128)(2,1)} %batch_ref.1, ...), custom_call_target="tpu_custom_call" | custom-call | tf_op jit(solution)/shard_map/pallas_call | solution.py:353
  35.4 1.9 %shard_map.95 = (bf16[128,2,512]{2,1,0:T(2,128)(2,1)}, bf16[128,2,512]{2,1,0:T(2,128)(2,1)}, bf16[128,2,512]{2,1,0:T(2,128)(2,1)}) custom-call(bf16[128,2,512]{2,1,0:T(2,128)(2,1)} %get-tuple-element.9.in_0, bf16[128,2,512]{2,1,0:T(2,128)(2,1)} %get-tuple-element.10.in_1, bf16[128,2,512]{2,1,0:T(2,128)(2,1)} %get-tuple-element.11.in_2), custom_call_target="tpu_custom_call" | custom-call | tf_op jit(solution)/shard_map/pallas_call | solution.py:376

commit v3 on v2

--- a/solution.py
+++ b/solution.py
@@ -129,8 +129,8 @@
     for index, source, edge_source in ((0, state_ref, head_ref), (1, state_ref, head_ref), (3, grad_ref, head_grad_ref)):
         init_start(index, source, edge_source, *down)
 
-    def forward_start():
-        for index in (5, 4):
+    def forward_start(halves=(5, 4)):
+        for index in halves:
             init_start(index, fwd_ref, batch_ref, *up)
     pl.when(home_here)(kern_remote.start)
 
@@ -154,7 +154,8 @@
 
     pl.when(home_here)(kern_local.wait)
     pl.when(jnp.logical_not(home_here))(kern_remote.wait_recv)
-    pl.when(jnp.logical_not(home_here))(forward_start)
+    pl.when(jnp.logical_not(jnp.logical_or(home_here, relays)))(forward_start)
+    pl.when(relays)(lambda: forward_start((5,)))
 
     def band(step, carry):
         which, b_off = step // 3, step % 3
@@ -242,13 +243,14 @@
 
     y1w[PAIR : 2 * PAIR] = arrived(0).astype(BF16)
     halo_start(*halos["y1"])
+    relay_on(1)
+    pl.when(relays)(lambda: forward_start((4,)))
     y2w[HALF : HALF + PAIR] = arrived(1).astype(BF16)
     halo_start(*halos["y2"])
-    relay_on(1)
+    relay_on(3)
     init_start(2, grad_ref, head_grad_ref, *down)
     g2w[HALF : HALF + PAIR] = arrived(3).astype(BF16)
     halo_start(*halos["g2"])
-    relay_on(3)
     x2w[PAIR : 2 * PAIR] = arrived(5).astype(BF16)
     halo_start(*halos["x2"])
 
@@ -332,15 +334,14 @@
         halo_done(*spec)
 
 
-def settle_kernel(in_0, in_1, in_2, out_0, out_1, out_2, buffer, sems):
-    reads = [pltpu.make_async_copy(ref, buffer.at[i], sems.at[0, i]) for i, ref in enumerate((in_0, in_1, in_2))]
-    writes = [pltpu.make_async_copy(buffer.at[i], ref, sems.at[1, i]) for i, ref in enumerate((out_0, out_1, out_2))]
-    for copy in reads:
+def settle_kernel(in_0, in_1, in_2, out_0, out_1, out_2, sems):
+    copies = [
+        pltpu.make_async_copy(source, target, sems.at[i])
+        for i, (source, target) in enumerate(((in_0, out_0), (in_1, out_1), (in_2, out_2)))
+    ]
+    for copy in copies:
         copy.start()
-    for read, write in zip(reads, writes):
-        read.wait()
-        write.start()
-    for copy in writes:
+    for copy in copies:
         copy.wait()
 
 
@@ -350,10 +351,11 @@
     field = lambda planes: pltpu.VMEM((planes * HALF, CELLS), BF16)
     dma = pltpu.SemaphoreType.DMA
     out = jax.ShapeDtypeStruct((PAIR, 2, CELLS), BF16)
+    fields = (fwd_states[0], back_states[0], back_grads[0], batch_in, head_state, head_grad, couplings[0])
     results = pl.pallas_call(
         functools.partial(step_kernel, n_section, n_slab),
         out_shape=(out, out, out),
-        in_specs=[anywhere] * 7,
+        in_specs=[pl.BlockSpec(memory_space=pltpu.HBM)] * 7,
         out_specs=(anywhere,) * 3,
         scratch_shapes=[
             pltpu.VMEM((6, HALF, 2, CELLS), BF16),
@@ -370,15 +372,16 @@
             pltpu.VMEM((6, HALF, 2, CELLS), BF16),
             dma((6,)), dma((6,)), dma((4,)), dma((4,)), dma((9, 2)), dma((9, 2)), dma((6,)), dma((6,)), dma((3,)),
         ],
-        compiler_params=pltpu.CompilerParams(collective_id=0, has_side_effects=True),
-    )(fwd_states[0], back_states[0], back_grads[0], batch_in, head_state, head_grad, couplings[0])
+        compiler_params=pltpu.CompilerParams(collective_id=0, has_side_effects=True, vmem_limit_bytes=32 << 20),
+    )(*(pltpu.with_memory_space_constraint(field, pltpu.HBM) for field in fields))
 
     settled = pl.pallas_call(
         settle_kernel,
         out_shape=(out, out, out),
         in_specs=[anywhere] * 3,
-        out_specs=(anywhere,) * 3,
-        scratch_shapes=[pltpu.VMEM((3, PAIR, 2, CELLS), BF16), dma((2, 3))],
+        out_specs=(pl.BlockSpec(memory_space=pltpu.HBM),) * 3,
+        scratch_shapes=[dma((3,))],
+        compiler_params=pltpu.CompilerParams(vmem_limit_bytes=4 << 20),
     )(*results)
     return tuple(value[None] for value in settled)
 

time: 37.4 us -> 36.6 us (0.979)
  Pallas kernels: 36.7 us -> 35.8 us
    pallas_call x1, Pallas kernels: 1.88 us -> 0.9 us  [shards(): pl.pallas_call(settle_kernel, out_shape=(out, out, out), in_specs=[anywhe...]
where the time goes in v3:
time: 36.6 us; the launch traced here: 36.5 us
  Pallas kernels  35.8 us (98%)
  between operations  0.64 us (2%)
    pallas_call x1, Pallas kernels, shards(): pl.pallas_call(functools.partial(step_kernel, n_section, n_slab), out_sha...  34.9 us
    pallas_call x1, Pallas kernels, shards(): pl.pallas_call(settle_kernel, out_shape=(out, out, out), in_specs=[anywhe...  0.9 us

profile of v3, /device:TPU:129, one launch (start us, length us, event | category | flops | bytes accessed | tf_op | source)
XLA Modules:
  0.0 36.5 jit_solution(10488242693608128088)
XLA Ops:
  0.6 34.9 %shard_map.94 = (bf16[128,2,512]{2,1,0:T(2,128)(2,1)S(1)}, bf16[128,2,512]{2,1,0:T(2,128)(2,1)S(1)}, bf16[128,2,512]{2,1,0:T(2,128)(2,1)S(1)}) custom-call(bf16[128,2,512]{2,1,0:T(2,128)(2,1)} %bitcast.8, bf16[128,2,512]{2,1,0:T(2,128)(2,1)} %bitcast.9, bf16[128,2,512]{2,1,0:T(2,128)(2,1)} %bitcast.10, bf16[128,2,512]{2,1,0:T(2,128)(2,1)} %batch_ref.1, ...), custom_call_target="tpu_custom_call" | custom-call | tf_op jit(solution)/shard_map/pallas_call | solution.py:355
  35.6 0.9 %shard_map.95 = (bf16[128,2,512]{2,1,0:T(2,128)(2,1)}, bf16[128,2,512]{2,1,0:T(2,128)(2,1)}, bf16[128,2,512]{2,1,0:T(2,128)(2,1)}) custom-call(bf16[128,2,512]{2,1,0:T(2,128)(2,1)S(1)} %get-tuple-element.9.in_0, bf16[128,2,512]{2,1,0:T(2,128)(2,1)S(1)} %get-tuple-element.10.in_1, bf16[128,2,512]{2,1,0:T(2,128)(2,1)S(1)} %get-tuple-element.11.in_2), custom_call_target="tpu_custom_call" | custom-call | tf_op jit(solution)/shard_map/pallas_call | solution.py:378

commit v4 on v3

--- a/solution.py
+++ b/solution.py
@@ -129,8 +129,8 @@
     for index, source, edge_source in ((0, state_ref, head_ref), (1, state_ref, head_ref), (3, grad_ref, head_grad_ref)):
         init_start(index, source, edge_source, *down)
 
-    def forward_start(halves=(5, 4)):
-        for index in halves:
+    def forward_start():
+        for index in (5, 4):
             init_start(index, fwd_ref, batch_ref, *up)
     pl.when(home_here)(kern_remote.start)
 
@@ -155,7 +155,6 @@
     pl.when(home_here)(kern_local.wait)
     pl.when(jnp.logical_not(home_here))(kern_remote.wait_recv)
     pl.when(jnp.logical_not(jnp.logical_or(home_here, relays)))(forward_start)
-    pl.when(relays)(lambda: forward_start((5,)))
 
     def band(step, carry):
         which, b_off = step // 3, step % 3
@@ -174,7 +173,11 @@
                 toep_t[where] = jnp.concatenate(order(line_t), 1)
         return carry
 
-    lax.fori_loop(0, 6 * PAIRS, band, 0)
+    def bands(first, last):
+        lax.fori_loop(first, last, band, 0)
+
+    pl.when(home_here)(lambda: bands(0, 6 * PAIRS))
+    pl.when(jnp.logical_not(home_here))(lambda: bands(0, 2 * PAIRS))
     pl.when(home_here)(forward_start)
 
     def halo(index, ref, width):
@@ -244,11 +247,13 @@
     y1w[PAIR : 2 * PAIR] = arrived(0).astype(BF16)
     halo_start(*halos["y1"])
     relay_on(1)
-    pl.when(relays)(lambda: forward_start((4,)))
+    pl.when(relays)(forward_start)
+    pl.when(jnp.logical_not(home_here))(lambda: bands(2 * PAIRS, 4 * PAIRS))
     y2w[HALF : HALF + PAIR] = arrived(1).astype(BF16)
     halo_start(*halos["y2"])
     relay_on(3)
     init_start(2, grad_ref, head_grad_ref, *down)
+    pl.when(jnp.logical_not(home_here))(lambda: bands(4 * PAIRS, 6 * PAIRS))
     g2w[HALF : HALF + PAIR] = arrived(3).astype(BF16)
     halo_start(*halos["g2"])
     x2w[PAIR : 2 * PAIR] = arrived(5).astype(BF16)

time: 36.6 us -> 37.3 us (1.019)
  the two profiles are of different devices: /device:TPU:129 before, /device:TPU:120 now
where the time goes in v4:
time: 37.3 us; the launch traced here: 37.2 us
  Pallas kernels  36.6 us (98%)
  between operations  0.64 us (2%)
    pallas_call x1, Pallas kernels, shards(): pl.pallas_call(functools.partial(step_kernel, n_section, n_slab), out_sha...  35.6 us
    pallas_call x1, Pallas kernels, shards(): pl.pallas_call(settle_kernel, out_shape=(out, out, out), in_specs=[anywhe...  0.9 us

profile of v4, /device:TPU:120, one launch (start us, length us, event | category | flops | bytes accessed | tf_op | source)
XLA Modules:
  0.0 37.2 jit_solution(17147699180675751341)
XLA Ops:
  0.6 35.6 %shard_map.94 = (bf16[128,2,512]{2,1,0:T(2,128)(2,1)S(1)}, bf16[128,2,512]{2,1,0:T(2,128)(2,1)S(1)}, bf16[128,2,512]{2,1,0:T(2,128)(2,1)S(1)}) custom-call(bf16[128,2,512]{2,1,0:T(2,128)(2,1)} %bitcast.8, bf16[128,2,512]{2,1,0:T(2,128)(2,1)} %bitcast.9, bf16[128,2,512]{2,1,0:T(2,128)(2,1)} %bitcast.10, bf16[128,2,512]{2,1,0:T(2,128)(2,1)} %batch_ref.1, ...), custom_call_target="tpu_custom_call" | custom-call | tf_op jit(solution)/shard_map/pallas_call | solution.py:360
  36.3 0.9 %shard_map.95 = (bf16[128,2,512]{2,1,0:T(2,128)(2,1)}, bf16[128,2,512]{2,1,0:T(2,128)(2,1)}, bf16[128,2,512]{2,1,0:T(2,128)(2,1)}) custom-call(bf16[128,2,512]{2,1,0:T(2,128)(2,1)S(1)} %get-tuple-element.9.in_0, bf16[128,2,512]{2,1,0:T(2,128)(2,1)S(1)} %get-tuple-element.10.in_1, bf16[128,2,512]{2,1,0:T(2,128)(2,1)S(1)} %get-tuple-element.11.in_2), custom_call_target="tpu_custom_call" | custom-call | tf_op jit(solution)/shard_map/pallas_call | solution.py:383
